TPU v7x, 512 devices: a whole 4x4x16 slice. The times are simulated.
512 devices in a mesh: mol: 128 (over z, y, core), traj: 4 (over x).
Axes of the slice: x: 4, y: 4, z: 16, core: 2. Of those that a mesh axis runs over, the one named last changes fastest.
Arguments:
- positions: float32 [64, 16384], P('traj', 'mol'), parts along dimension 0, may hold values from -1.2 to 1.2
- velocities: float32 [64, 16384], P('traj', 'mol'), parts along dimension 0, may hold values from -3 to 3
- amplitudes: float32 [4096, 64], P('mol', 'traj'), parts along dimension 1, may hold values from -6 to 6
- momenta: float32 [4096, 64], P('mol', 'traj'), parts along dimension 1, may hold values from -6 to 6
- sites: int32 [16384], P('mol'), may hold values from 0 to 32767
- wavevectors: int32 [4096], replicated, may hold values from 1 to 32767
- mode_freq: float32 [4096], P('mol'), may hold values from 0.5 to 2
- coupling: float32 [4096], P('mol'), may hold values from 0.0078125 to 0.03125
- depth: float32 [16384], P('mol'), may hold values from 0.5 to 2
- stiffness: float32 [16384], P('mol'), may hold values from 0.8 to 1.5
- dipole_slope: float32 [16384], P('mol'), may hold values from -4 to 4
Outputs:
- final_positions: float32 [64, 16384], P('traj', 'mol'), parts along dimension 0
- final_velocities: float32 [64, 16384], P('traj', 'mol'), parts along dimension 0
- final_amplitudes: float32 [4096, 64], P('mol', 'traj'), parts along dimension 1
- final_momenta: float32 [4096, 64], P('mol', 'traj'), parts along dimension 1
There are 4 independent parts, one for each index of `traj`. A program takes and returns all parts, laid end to end along the dimension named above; an argument that names none is the same for every part. Nothing has to cross between parts.
All inputs are finite; a program needn't handle non-finite values.
Results may differ from a plain program's by a relative error of at most 0.0003.
Values sent between devices are 32-bit elements; how exact they have to be, the bound alone decides.
No kernel may reach another device: no remote copies, remote signals or barrier semaphores. Data moves between devices by JAX's collectives and lax.ppermute only.
A program may use at most 64 MiB of HBM per device.

v0:
```python
import math
import jax
import jax.numpy as jnp
from jax import lax
from jax.sharding import PartitionSpec as P

STEPS = 2


def phase_tile(waves, sites, lattice):
    high = sites // 256
    low = sites % 256
    first = waves[:, None] * high[None, :] % lattice
    residue = (first * 256 + waves[:, None] * low[None, :]) % lattice
    angle = residue.astype(jnp.float32) * (2.0 * math.pi / lattice)
    return jnp.sin(angle)


def project_dipole(tile, dipole):
    return lax.dot_general(
        tile,
        dipole,
        (((1,), (1,)), ((), ())),
        precision=lax.Precision.HIGHEST,
        preferred_element_type=jnp.float32,
    )


def project_modes(weighted, tile):
    return lax.dot_general(
        weighted,
        tile,
        (((0,), (0,)), ((), ())),
        precision=lax.Precision.HIGHEST,
        preferred_element_type=jnp.float32,
    )


def advance_bonds(positions, velocities, pull, depth, stiffness, dipole_slope, step_time):
    damped = jnp.exp(-stiffness[None, :] * positions)
    force = (
        -2.0 * depth[None, :] * stiffness[None, :] * (1.0 - damped) * damped
        - dipole_slope[None, :] * pull
    )
    velocities = velocities + step_time * force
    positions = positions + step_time * velocities
    return (positions, velocities)


def local(
    positions,
    velocities,
    amplitudes,
    momenta,
    sites,
    wavevectors,
    mode_freq,
    coupling,
    depth,
    stiffness,
    dipole_slope,
):
    step_time = 0.2
    lattice = 2 * sites.shape[0] * lax.axis_size("mol")
    owned_rows = amplitudes.shape[0]
    stored = phase_tile(wavevectors, sites, lattice)

    def tile_rows():
        return stored

    for step in range(STEPS):
        dipole = dipole_slope[None, :] * positions

        def drive_term(start, count, dipole=dipole):
            return project_dipole(tile_rows(), dipole)

        drive = lax.psum_scatter(
            drive_term(jnp.int32(0), lax.axis_size("mol") * owned_rows),
            "mol",
            scatter_dimension=0,
            tiled=True,
        )
        momenta = momenta + step_time * (
            -(mode_freq * mode_freq)[:, None] * amplitudes - coupling[:, None] * drive
        )
        amplitudes = amplitudes + step_time * momenta
        weighted = coupling[:, None] * amplitudes
        pull = project_modes(lax.all_gather(weighted, "mol", axis=0, tiled=True), tile_rows())
        positions, velocities = advance_bonds(
            positions, velocities, pull, depth, stiffness, dipole_slope, step_time
        )
    return (positions, velocities, amplitudes, momenta)


def solution(mesh):
    return jax.shard_map(
        local,
        mesh=mesh,
        in_specs=(
            P("traj", "mol"),
            P("traj", "mol"),
            P("mol", "traj"),
            P("mol", "traj"),
            P("mol"),
            P(),
            P("mol"),
            P("mol"),
            P("mol"),
            P("mol"),
            P("mol"),
        ),
        out_specs=(P("traj", "mol"), P("traj", "mol"), P("mol", "traj"), P("mol", "traj")),
        check_vma=False,
    )
```

profile of v0, /device:TPU:1, one launch (start us, length us, event | category | flops | bytes accessed | tf_op | source)
XLA Modules:
  0.0 796.6 jit_solution(9365872709216338628)
XLA Ops:
  7.2 0.0 reduce-scatter.7.cloned.1.call-start
  7.2 0.7 and_select_fusion.1
  7.9 13.8 %fusion.17 = f32[4096,16]{1,0:T(8,128)} fusion(s32[128]{0:T(128)S(1)} %get-tuple-element.10, s32[128]{0:T(128)S(1)} %get-tuple-element.9, s32[4096]{0:T(1024)} %param.16, f32[16,128]{1,0:T(8,128)} %param.11, f32[128]{0:T(128)} %param.21), kind=kOutput, calls=%fused_computation.24 | convolution fusion | flops 115345408 | bytes 288256
  21.7 0.0 copy-start
  21.7 0.0 reduce-scatter.7.cloned.1.call-update
  21.7 0.0 reduce-scatter.9.cloned.1.call-start
  21.8 0.5 copy-done.8
  22.3 0.0 copy-done.3
  22.3 0.0 copy-done.4
  22.3 257.0 %reduce-scatter.7.cloned.1.call-done = f32[32,16]{1,0:T(8,128)} async-done(((f32[4096,16]{1,0:T(8,128)}), f32[32,16]{1,0:T(8,128)}) %reduce-scatter.7.cloned.1.call-update) | async-done | bytes 2064
  279.3 0.8 copy.20
  280.2 111.7 %all-gather = f32[128,32,16]{1,2,0:T(8,128)S(1)} all-gather(f32[1,32,16]{1,2,0:T(8,128)S(1)} %multiply_bitcast_fusion.1), channel_id=1, replica_groups=mesh['mol'=128,'traj'=4] {'mol'}, dimensions={0}, use_global_device_ids=true | all-gather | bytes 264192 | tf_op jit(solution)/shard_map/all_gather | solution.py:88
  391.9 0.3 copy.17
  392.2 0.5 reshape.21
  392.8 10.0 %fusion.12 = f32[16,128]{1,0:T(8,128)S(1)} fusion(f32[16,128]{1,0:T(8,128)S(1)} %copy-done.6, f32[4096,16]{0,1:T(8,128)S(1)} %reshape.21, s32[128]{0:T(128)S(1)} %get-tuple-element.10, s32[128]{0:T(128)S(1)} %get-tuple-element.9, s32[4096]{0:T(1024)S(1)} %copy-done.5, f32[16,128]{1,0:T(8,128)S(1)} %copy-done.7, f32[128]{0:T(128)S(1)} %copy-done.9, ...), kind=kOutput, calls=%fused_computation.22 | convolution fusion | flops 115359744 | bytes 305664 | tf_op jit(solution)/shard_map/dot_general | solution.py:30
  402.8 13.3 %fusion.14 = f32[4096,16]{1,0:T(8,128)} fusion(s32[128]{0:T(128)S(1)} %get-tuple-element.10, s32[128]{0:T(128)S(1)} %get-tuple-element.9, s32[4096]{0:T(1024)S(1)} %copy-done.5, f32[128]{0:T(128)S(1)} %copy-done.9, f32[16,128]{1,0:T(8,128)S(1)} %copy-done.7, f32[16,128]{1,0:T(8,128)S(1)} %fusion.12), kind=kOutput, calls=%fused_computation.23 | convolution fusion | flops 115349504 | bytes 296448
  416.1 0.0 reduce-scatter.9.cloned.1.call-update
  416.1 249.2 %reduce-scatter.9.cloned.1.call-done = f32[32,16]{1,0:T(8,128)} async-done(((f32[4096,16]{1,0:T(8,128)}), f32[32,16]{1,0:T(8,128)}) %reduce-scatter.9.cloned.1.call-update) | async-done | bytes 2064
  665.3 0.8 copy.22
  666.1 0.6 multiply_bitcast_fusion
  666.7 111.6 %all-gather.1 = f32[128,32,16]{1,2,0:T(8,128)S(1)} all-gather(f32[1,32,16]{1,2,0:T(8,128)S(1)} %get-tuple-element.4), channel_id=1, replica_groups=mesh['mol'=128,'traj'=4] {'mol'}, dimensions={0}, use_global_device_ids=true | all-gather | bytes 264192 | tf_op jit(solution)/shard_map/all_gather | solution.py:88
  778.2 0.3 copy.18
  778.6 0.5 reshape.23
  779.1 10.7 %multiply_add_fusion = (f32[16,128]{1,0:T(8,128)}, f32[16,128]{1,0:T(8,128)}) fusion(f32[16,128]{1,0:T(8,128)S(1)} %copy-done.7, f32[16,128]{1,0:T(8,128)S(1)} %fusion.12, f32[4096,16]{0,1:T(8,128)S(1)} %reshape.23, s32[128]{0:T(128)S(1)} %get-tuple-element.10, s32[128]{0:T(128)S(1)} %get-tuple-element.9, s32[4096]{0:T(1024)S(1)} %copy-done.5, ...), kind=kOutput, calls=%fused_computation.25 | convolution fusion | flops 115367936 | bytes 313856 | tf_op jit(solution)/shard_map/dot_general | solution.py:30
  (19 shorter events, 0.1 us)
Async XLA Ops:
  7.2 272.2 %reduce-scatter.7.cloned.1.call-start = ((), (), s32[]{:S(2)}) async-start(), calls=%async_computation.2 | async-start | bytes 2113536
  21.7 0.7 copy-start.8
  21.7 0.7 copy-start.3
  21.7 0.7 copy-start.4
  21.7 258.5 %copy-start = (f32[32,16]{0,1:T(8,128)S(1)}, f32[32,16]{0,1:T(8,128)}, u32[]{:S(2)}) copy-start(f32[32,16]{0,1:T(8,128)} %param.13) | copy-start | bytes 6148
  21.7 258.4 %copy-start.1 = (f32[32,16]{0,1:T(8,128)S(1)}, f32[32,16]{0,1:T(8,128)}, u32[]{:S(2)}) copy-start(f32[32,16]{0,1:T(8,128)} %param.14) | copy-start | bytes 6148
  21.7 258.4 %copy-start.2 = (f32[32]{0:T(128)S(1)}, f32[32]{0:T(128)}, u32[]{:S(2)}) copy-start(f32[32]{0:T(128)} %param.18) | copy-start | bytes 388
  21.7 643.5 %reduce-scatter.9.cloned.1.call-start = ((), (), s32[]{:S(2)}) async-start(), calls=%async_computation.3 | async-start | bytes 2113536
  280.1 112.6 %copy-start.5 = (s32[4096]{0:T(1024)S(1)}, s32[4096]{0:T(1024)}, u32[]{:S(2)}) copy-start(s32[4096]{0:T(1024)} %param.16) | copy-start | bytes 49156
  280.2 112.6 %copy-start.6 = (f32[16,128]{1,0:T(8,128)S(1)}, f32[16,128]{1,0:T(8,128)}, u32[]{:S(2)}) copy-start(f32[16,128]{1,0:T(8,128)} %param.12) | copy-start | bytes 24580
  280.2 112.6 %copy-start.7 = (f32[16,128]{1,0:T(8,128)S(1)}, f32[16,128]{1,0:T(8,128)}, u32[]{:S(2)}) copy-start(f32[16,128]{1,0:T(8,128)} %param.11) | copy-start | bytes 24580
  280.2 112.6 %copy-start.9 = (f32[128]{0:T(128)S(1)}, f32[128]{0:T(128)}, u32[]{:S(2)}) copy-start(f32[128]{0:T(128)} %param.21) | copy-start | bytes 1540
Sparse Core Ops, SparseCore 0:
  21.8 257.4 reduce-scatter.6
  416.2 248.9 reduce-scatter.8
where the time goes:
time: 797 us
  waiting for transfers between devices  506 us (63%)
  blocking collectives  223 us (28%)
  matrix products  47.8 us (6%)
  between operations  14.2 us (2%)
    unnamed x4, waiting for transfers between devices  506 us
    all_gather x2, blocking collectives, local(): lax.all_gather(weighted, 'mol', axis=0, tiled=True)  223 us
    unnamed x2, matrix products  27 us
    dot_general x2, matrix products, project_modes(): lax.dot_general(weighted, tile, (((0,), (0,)), ((), ())), precision=lax.P...  20.8 us
  transfers between devices with their start and end apart: 2, of which 2 were waited for; matrix products, arithmetic and copies ran while one was open for 0% of the time, Pallas kernels for 0%

commit v1 on v0

--- a/solution.py
+++ b/solution.py
@@ -5,6 +5,13 @@
 from jax.sharding import PartitionSpec as P
 
 STEPS = 2
+
+
+def exchange_gather(x, axis, d):
+    size = lax.axis_size(axis)
+    tiles = jnp.stack([x for _ in range(size)])
+    tiles = lax.all_to_all(tiles, axis, split_axis=0, concat_axis=0)
+    return jnp.concatenate(tiles, axis=d)
 
 
 def phase_tile(waves, sites, lattice):
@@ -85,7 +92,7 @@
         )
         amplitudes = amplitudes + step_time * momenta
         weighted = coupling[:, None] * amplitudes
-        pull = project_modes(lax.all_gather(weighted, "mol", axis=0, tiled=True), tile_rows())
+        pull = project_modes(exchange_gather(weighted, "mol", 0), tile_rows())
         positions, velocities = advance_bonds(
             positions, velocities, pull, depth, stiffness, dipole_slope, step_time
         )

time: 797 us -> 665 us (0.83)
  blocking collectives: 223 us -> 44.3 us
  starting transfers between devices: 0.08 us -> 24.2 us
  waiting for transfers between devices: 506 us -> 522 us
    all_gather x2 -> x0, blocking collectives: 223 us -> none  [local(): lax.all_gather(weighted, 'mol', axis=0, tiled=True)]
    all_to_all x0 -> x1, blocking collectives: none -> 44.3 us  [exchange_gather(): tiles = lax.all_to_all(tiles, axis, split_axis=0, concat_axis=0)]
    all_to_all x0 -> x1, starting transfers between devices: none -> 23.9 us  [exchange_gather(): tiles = lax.all_to_all(tiles, axis, split_axis=0, concat_axis=0)]
    all_to_all x0 -> x1, waiting for transfers between devices: none -> 20.2 us  [exchange_gather(): tiles = lax.all_to_all(tiles, axis, split_axis=0, concat_axis=0)]
  transfers between devices with their start and end apart: 2 -> 3, of which waited for: 2 -> 3; matrix products, arithmetic and copies ran while one was open for 0% -> 0% of each run, Pallas kernels for 0% -> 0%
where the time goes in v1:
time: 665 us; the launch traced here: 663 us
  waiting for transfers between devices  522 us (78%)
  matrix products  47.6 us (7%)
  blocking collectives  44.3 us (7%)
  starting transfers between devices  24.2 us (4%)
  between operations  14.2 us (2%)
  local copies, waits for them, and re-layouts  6.68 us (1%)
    unnamed x4, waiting for transfers between devices  502 us
    all_to_all x1, blocking collectives, exchange_gather(): tiles = lax.all_to_all(tiles, axis, split_axis=0, concat_axis=0)  44.3 us
    unnamed x2, matrix products  27 us
    all_to_all x1, starting transfers between devices, exchange_gather(): tiles = lax.all_to_all(tiles, axis, split_axis=0, concat_axis=0)  23.9 us
    dot_general x2, matrix products, project_modes(): lax.dot_general(weighted, tile, (((0,), (0,)), ((), ())), precision=lax.P...  20.6 us
    all_to_all x1, waiting for transfers between devices, exchange_gather(): tiles = lax.all_to_all(tiles, axis, split_axis=0, concat_axis=0)  20.2 us
  transfers between devices with their start and end apart: 3, of which 3 were waited for; matrix products, arithmetic and copies ran while one was open for 0% of the time, Pallas kernels for 0%

profile of v1, /device:TPU:1, one launch (start us, length us, event | category | flops | bytes accessed | tf_op | source)
XLA Modules:
  0.0 663.3 jit_solution(4919036158424393569)
XLA Ops:
  7.2 0.7 and_select_fusion.1
  7.9 13.8 %fusion.17 = f32[4096,16]{1,0:T(8,128)} fusion(s32[128]{0:T(128)S(1)} %get-tuple-element.10, s32[128]{0:T(128)S(1)} %get-tuple-element.9, s32[4096]{0:T(1024)} %param.16, f32[16,128]{1,0:T(8,128)} %param.11, f32[128]{0:T(128)} %param.21), kind=kOutput, calls=%fused_computation.24 | convolution fusion | flops 115345408 | bytes 288256
  21.7 0.6 copy-done.8
  22.3 257.0 %reduce-scatter.7.cloned.1.call-done = f32[32,16]{1,0:T(8,128)} async-done(((f32[4096,16]{1,0:T(8,128)}), f32[32,16]{1,0:T(8,128)}) %reduce-scatter.7.cloned.1.call-update) | async-done | bytes 2064
  279.3 0.8 copy.20
  280.2 1.2 reshape.36
  281.4 23.9 %all-to-all-start = ((f32[128,1,512]{2,1,0:T(1,128)}), f32[128,1,512]{2,1,0:T(1,128)S(1)}, u32[]{:S(2)}, u32[]{:S(2)}) async-start(f32[128,1,512]{2,1,0:T(1,128)} %reshape.36), calls=%async_computation | async-start | bytes 524288 | tf_op jit(solution)/shard_map/all_to_all | solution.py:13
  305.6 20.2 %all-to-all-done = f32[128,1,512]{2,1,0:T(1,128)S(1)} async-done(((f32[128,1,512]{2,1,0:T(1,128)}), f32[128,1,512]{2,1,0:T(1,128)S(1)}, u32[]{:S(2)}, u32[]{:S(2)}) %all-to-all-start) | async-done | bytes 262176 | tf_op jit(solution)/shard_map/all_to_all | solution.py:13
  325.7 0.5 broadcast.102
  326.2 1.3 reduce
  327.6 0.3 reshape.37
  327.8 0.3 copy.17
  328.2 0.5 reshape.30
  328.7 10.1 %fusion.12 = f32[16,128]{1,0:T(8,128)S(1)} fusion(f32[16,128]{1,0:T(8,128)S(1)} %copy-done.6, f32[4096,16]{0,1:T(8,128)S(1)} %reshape.30, s32[128]{0:T(128)S(1)} %get-tuple-element.10, s32[128]{0:T(128)S(1)} %get-tuple-element.9, s32[4096]{0:T(1024)S(1)} %copy-done.5, f32[16,128]{1,0:T(8,128)S(1)} %copy-done.7, f32[128]{0:T(128)S(1)} %copy-done.9, ...), kind=kOutput, calls=%fused_computation.22 | convolution fusion | flops 115359744 | bytes 305664 | tf_op jit(solution)/shard_map/dot_general | solution.py:37
  338.8 13.3 %fusion.14 = f32[4096,16]{1,0:T(8,128)} fusion(s32[128]{0:T(128)S(1)} %get-tuple-element.10, s32[128]{0:T(128)S(1)} %get-tuple-element.9, s32[4096]{0:T(1024)S(1)} %copy-done.5, f32[128]{0:T(128)S(1)} %copy-done.9, f32[16,128]{1,0:T(8,128)S(1)} %copy-done.7, f32[16,128]{1,0:T(8,128)S(1)} %fusion.12), kind=kOutput, calls=%fused_computation.23 | convolution fusion | flops 115349504 | bytes 296448
  352.1 245.2 %reduce-scatter.9.cloned.1.call-done = f32[32,16]{1,0:T(8,128)} async-done(((f32[4096,16]{1,0:T(8,128)}), f32[32,16]{1,0:T(8,128)}) %reduce-scatter.9.cloned.1.call-update) | async-done | bytes 2064
  597.3 0.8 copy.22
  598.1 0.6 broadcast_multiply_fusion
  598.8 0.5 reshape.38
  599.2 44.3 %all_to_all.10 = f32[128,1,512]{2,1,0:T(1,128)S(1)} all-to-all(f32[128,1,512]{2,1,0:T(1,128)S(1)} %reshape.38), channel_id=1, replica_groups=mesh['mol'=128,'traj'=4] {'mol'}, dimensions={0} | all-to-all | bytes 524288 | tf_op jit(solution)/shard_map/all_to_all | solution.py:13
  643.6 1.3 reduce.1
  645.1 0.3 copy.18
  645.5 0.5 reshape.31
  645.9 10.5 %multiply_add_fusion = (f32[16,128]{1,0:T(8,128)}, f32[16,128]{1,0:T(8,128)}) fusion(f32[16,128]{1,0:T(8,128)S(1)} %copy-done.7, f32[16,128]{1,0:T(8,128)S(1)} %fusion.12, f32[4096,16]{0,1:T(8,128)S(1)} %reshape.31, s32[128]{0:T(128)S(1)} %get-tuple-element.10, s32[128]{0:T(128)S(1)} %get-tuple-element.9, s32[4096]{0:T(1024)S(1)} %copy-done.5, ...), kind=kOutput, calls=%fused_computation.25 | convolution fusion | flops 115367936 | bytes 313856 | tf_op jit(solution)/shard_map/dot_general | solution.py:37
  (29 shorter events, 0.8 us)
Async XLA Ops:
  7.2 272.2 %reduce-scatter.7.cloned.1.call-start = ((), (), s32[]{:S(2)}) async-start(), calls=%async_computation.4 | async-start | bytes 2113536
  21.7 0.7 copy-start.8
  21.7 258.5 %copy-start = (f32[32,16]{0,1:T(8,128)S(1)}, f32[32,16]{0,1:T(8,128)}, u32[]{:S(2)}) copy-start(f32[32,16]{0,1:T(8,128)} %param.13) | copy-start | bytes 6148
  21.7 258.5 %copy-start.1 = (f32[32,16]{0,1:T(8,128)S(1)}, f32[32,16]{0,1:T(8,128)}, u32[]{:S(2)}) copy-start(f32[32,16]{0,1:T(8,128)} %param.14) | copy-start | bytes 6148
  21.7 258.5 %copy-start.2 = (f32[32]{0:T(128)S(1)}, f32[32]{0:T(128)}, u32[]{:S(2)}) copy-start(f32[32]{0:T(128)} %param.18) | copy-start | bytes 388
  21.7 283.8 %copy-start.3 = (f32[128]{0:T(128)S(1)}, f32[128]{0:T(128)}, u32[]{:S(2)}) copy-start(f32[128]{0:T(128)} %param.20) | copy-start | bytes 1540
  21.7 283.8 %copy-start.4 = (f32[128]{0:T(128)S(1)}, f32[128]{0:T(128)}, u32[]{:S(2)}) copy-start(f32[128]{0:T(128)} %param.19) | copy-start | bytes 1540
  281.4 44.3 %all-to-all-start = ((f32[128,1,512]{2,1,0:T(1,128)}), f32[128,1,512]{2,1,0:T(1,128)S(1)}, u32[]{:S(2)}, u32[]{:S(2)}) async-start(f32[128,1,512]{2,1,0:T(1,128)} %reshape.36), calls=%async_computation | async-start | bytes 524288 | tf_op jit(solution)/shard_map/all_to_all | solution.py:13
  305.3 292.0 %reduce-scatter.9.cloned.1.call-start = ((), (), s32[]{:S(2)}) async-start(), calls=%async_computation.5 | async-start | bytes 2113536
  327.5 1.2 copy-start.5
  327.5 1.2 copy-start.6
  327.5 1.2 copy-start.7
  327.5 1.2 copy-start.9
Sparse Core Ops, SparseCore 0:
  21.8 257.4 reduce-scatter.6
  352.2 245.0 reduce-scatter.8
